TPU v7x, 256 devices: a whole 4x4x8 slice. The times are simulated.
256 devices in a mesh: ctx: 32 (over y, x, core), head: 8 (over z).
Axes of the slice: x: 4, y: 4, z: 8, core: 2. Of those that a mesh axis runs over, the one named last changes fastest.
Arguments:
- query_rows: bfloat16 [32768, 4096], P('ctx', 'head'), may hold values from -6 to 6
- key_rows: bfloat16 [32768, 4096], P('ctx', 'head'), may hold values from -6 to 6
- value_rows: bfloat16 [32768, 4096], P('ctx', 'head'), may hold values from -6 to 6
- frequencies: bfloat16 [32, 128, 128], P('head'), may hold values from -4.1875 to 4.1875
- norm_gain: bfloat16 [4096], P('head'), may hold values from 0.25 to 1.75
- out_weight: bfloat16 [4096, 4096], P(None, 'head'), may hold values from -0.09375 to 0.09375
Outputs:
- projected: bfloat16 [32768, 4096], P('ctx', 'head')
All inputs are finite; a program needn't handle non-finite values.
Results may differ from a plain program's by a relative error of at most 0.009.
Values may be sent and summed in bfloat16 or wider, within the bound.
A program may use at most 128 MiB of HBM per device.

v0:
```python
import math

import jax
import jax.numpy as jnp
from jax import lax
from jax.sharding import PartitionSpec as P


def carried_in(value, axis, join, neutral):
    count, mine = (lax.axis_size(axis), lax.axis_index(axis))
    pieces = lax.all_gather(value, axis)
    subtotal = jnp.full_like(value, 0) + jnp.asarray(neutral, value.dtype)

    def turn(position, subtotal):
        longer = join(subtotal, pieces[position])
        return jnp.where(position < mine, longer, subtotal)

    return lax.fori_loop(0, count - 1, turn, subtotal)


def features_of(inputs, frequencies, freq_count):
    phases = jnp.einsum("bthd,hdf->bthf", inputs, frequencies, preferred_element_type=jnp.float32)
    joined = jnp.concatenate([jnp.cos(phases), jnp.sin(phases)], axis=-1)
    return (joined * (1.0 / math.sqrt(freq_count))).astype(jnp.bfloat16)


def add_states(first_part, second_part):
    return first_part + second_part


def local(query_rows, key_rows, value_rows, frequencies, norm_gain, out_weight):
    row_count = query_rows.shape[0]
    heads_here, head_width, freq_count = frequencies.shape
    span_rows = min(512, row_count)
    span_count = row_count // span_rows
    span_shape = (span_count, span_rows, heads_here, head_width)
    query_spans = query_rows.reshape(span_shape)
    key_spans = key_rows.reshape(span_shape)
    value_spans = value_rows.reshape(span_shape)
    query_feat = features_of(query_spans, frequencies, freq_count)
    key_feat = features_of(key_spans, frequencies, freq_count)
    span_states = jnp.einsum(
        "bthf,bthd->bhfd", key_feat, value_spans, preferred_element_type=jnp.float32
    )
    shard_total = jnp.sum(span_states, axis=0)
    preceding = carried_in(shard_total, "ctx", add_states, jnp.zeros_like(shard_total))
    running_sums = jnp.cumsum(span_states, axis=0)
    earlier_local = jnp.concatenate([jnp.zeros_like(span_states[:1]), running_sums[:-1]], axis=0)
    carried_low = (preceding[None] + earlier_local).astype(jnp.bfloat16)
    causal = jnp.arange(span_rows)[:, None] >= jnp.arange(span_rows)[None, :]
    scores = jnp.einsum("bthf,bshf->bhts", query_feat, key_feat, preferred_element_type=jnp.float32)
    scores = jnp.where(causal[None, None], scores, jnp.zeros_like(scores)).astype(jnp.bfloat16)
    local_part = jnp.einsum(
        "bhts,bshd->bthd", scores, value_spans, preferred_element_type=jnp.float32
    )
    prior_part = jnp.einsum(
        "bthf,bhfd->bthd", query_feat, carried_low, preferred_element_type=jnp.float32
    )
    attended = local_part + prior_part
    gain_table = norm_gain.astype(jnp.float32).reshape(heads_here, head_width)
    mean_square = jnp.mean(attended * attended, axis=-1, keepdims=True)
    normed = (attended * lax.rsqrt(mean_square + 1e-06) * gain_table[None, None]).astype(
        jnp.bfloat16
    )
    normed = normed.reshape(row_count, heads_here * head_width)
    projected = jnp.dot(
        lax.all_gather(normed, "head", axis=1, tiled=True),
        out_weight,
        preferred_element_type=jnp.float32,
    )
    return projected.astype(jnp.bfloat16)


def solution(mesh):
    return jax.shard_map(
        local,
        mesh=mesh,
        in_specs=(
            P("ctx", "head"),
            P("ctx", "head"),
            P("ctx", "head"),
            P("head", None, None),
            P("head"),
            P(None, "head"),
        ),
        out_specs=P("ctx", "head"),
        check_vma=False,
    )
```

profile of v0, /device:TPU:1, one launch (start us, length us, event | category | flops | bytes accessed | tf_op | source)
XLA Modules:
  0.0 270.1 jit_solution(10711758108041598171)
XLA Ops:
  6.5 0.0 copy-start
  6.5 0.0 copy-start.2
  6.5 0.0 all-gather.6.cloned.1.call-start
  6.5 1.4 reshape.34
  8.0 0.1 copy-done.2
  8.1 0.3 reshape.35
  8.4 0.0 copy-done
  8.4 9.7 %cosine_bitcast_fusion.1 = (f32[2,512,4,128]{1,3,0,2:T(8,128)}, f32[2,512,4,128]{1,3,0,2:T(8,128)}) fusion(bf16[2,512,4,128]{3,2,1,0:T(4,128)(2,1)S(1)} %reshape.34, bf16[4,128,128]{2,1,0:T(8,128)(2,1)S(1)} %copy-done), kind=kOutput, calls=%fused_computation.16 | convolution fusion | flops 134217728 | bytes 5373952 | tf_op jit(solution)/shard_map/bthd,hdf->bthf/dot_general | solution.py:22
  18.1 0.0 copy-start.3
  18.1 9.7 %cosine_bitcast_fusion = (f32[2,512,4,128]{1,3,0,2:T(8,128)}, f32[2,512,4,128]{1,3,0,2:T(8,128)}) fusion(bf16[2,512,4,128]{3,2,1,0:T(4,128)(2,1)S(1)} %reshape.35, bf16[4,128,128]{2,1,0:T(8,128)(2,1)S(1)} %copy-done), kind=kOutput, calls=%fused_computation.14 | convolution fusion | flops 134217728 | bytes 5373952 | tf_op jit(solution)/shard_map/bthd,hdf->bthf/dot_general | solution.py:22
  27.9 0.0 copy-done.3
  27.9 0.3 reshape.36
  28.2 0.0 copy-start.4
  28.2 4.4 %fusion.1 = (bf16[2,512,4,256]{1,3,0,2:T(8,128)(2,1)S(1)}, bf16[2,512,4,256]{1,3,0,2:T(8,128)(2,1)S(1)}) fusion(f32[2,512,4,128]{1,3,0,2:T(8,128)} %get-tuple-element.109, f32[2,512,4,128]{1,3,0,2:T(8,128)} %get-tuple-element.108, f32[2,512,4,128]{1,3,0,2:T(8,128)} %get-tuple-element.111, f32[2,512,4,128]{1,3,0,2:T(8,128)} %get-tuple-element.110), kind=kLoop, calls=%fused_computation.4 | loop fusion | flops 6291456 | bytes 12582912 | tf_op jit(solution)/shard_map/convert_element_type | solution.py:24
  32.6 0.0 copy-start.1
  32.6 0.0 copy-done.4
  32.6 2.5 fusion.28
  35.1 0.0 copy-done.1
  35.1 0.0 all-gather.6.cloned.1.call-update
  35.2 0.0 all-gather.4.cloned.1.call-start
  35.2 1.3 fusion.37
  36.6 0.1 iota_compare_fusion
  36.7 0.0 copy-done.5
  36.7 5.8 %fusion = f32[2,4,512,128]{2,3,1,0:T(8,128)} fusion(pred[512,512]{1,0:T(8,128)(4,1)S(1)} %iota_compare_fusion, bf16[2,512,4,256]{1,3,0,2:T(8,128)(2,1)} %copy-done.1, bf16[2,512,4,256]{1,3,0,2:T(8,128)(2,1)S(1)} %get-tuple-element.116, bf16[2,512,4,128]{3,2,1,0:T(4,128)(2,1)} %copy-done.4), kind=kOutput, calls=%fused_computation.2 | convolution fusion | flops 1614807040 | bytes 7602176 | tf_op jit(solution)/shard_map/bhts,bshd->bthd/dot_general | solution.py:53
  42.5 74.5 %all-gather.6.cloned.1.call-done = f32[128,256,128]{2,1,0:T(8,128)} async-done(((f32[4,256,128]{2,1,0:T(8,128)}), f32[128,256,128]{2,1,0:T(8,128)}) %all-gather.6.cloned.1.call-update) | async-done | bytes 16777232 | tf_op jit(solution)/shard_map/all_gather | solution.py:11
  117.0 38.4 %while.14 = (s32[]{:T(128)}, f32[4,256,128]{2,1,0:T(8,128)S(1)}, s32[]{:T(128)}, f32[32,4,256,128]{3,2,1,0:T(8,128)}, s32[]{:T(128)}, /*index=5*/s32[]{:T(128)}) while((s32[]{:T(128)}, f32[4,256,128]{2,1,0:T(8,128)S(1)}, s32[]{:T(128)}, f32[32,4,256,128]{3,2,1,0:T(8,128)}, s32[]{:T(128)}, /*index=5*/s32[]{:T(128)}) %tuple.44), condition=%wide.region_2.3_spmd.clone, body=%wide.region_1.2_spmd.clone.sunk | while | flops 393220 | bytes 1572957 | solution.py:18
  117.0 1.2 add_select_fusion.2
  118.3 1.2 add_select_fusion.2
  119.5 1.2 add_select_fusion.2
  120.7 1.2 add_select_fusion.2
  122.0 1.2 add_select_fusion.2
  123.2 1.2 add_select_fusion.2
  124.5 1.2 add_select_fusion.2
  125.7 1.2 add_select_fusion.2
  126.9 1.2 add_select_fusion.2
  128.2 1.2 add_select_fusion.2
  129.4 1.2 add_select_fusion.2
  130.7 1.2 add_select_fusion.2
  131.9 1.2 add_select_fusion.2
  133.1 1.2 add_select_fusion.2
  134.4 1.2 add_select_fusion.2
  135.6 1.2 add_select_fusion.2
  136.9 1.2 add_select_fusion.2
  138.1 1.2 add_select_fusion.2
  139.3 1.2 add_select_fusion.2
  140.6 1.2 add_select_fusion.2
  141.8 1.2 add_select_fusion.2
  143.1 1.2 add_select_fusion.2
  144.3 1.2 add_select_fusion.2
  145.5 1.2 add_select_fusion.2
  146.8 1.2 add_select_fusion.2
  148.0 1.2 add_select_fusion.2
  149.3 1.2 add_select_fusion.2
  150.5 1.2 add_select_fusion.2
  151.7 1.2 add_select_fusion.2
  153.0 1.2 add_select_fusion.2
  154.2 1.2 add_select_fusion.2
  155.5 2.2 multiply_reduce_fusion
  157.6 0.3 multiply_convert_fusion
  157.9 0.8 copy.37
  158.7 1.2 copy.83
  159.8 0.0 all-gather.4.cloned.1.call-update
  159.8 93.4 %all-gather.4.cloned.1.call-done = bf16[1024,4096]{1,0:T(8,128)(2,1)} async-done(((bf16[1024,512]{1,0:T(8,128)(2,1)}), bf16[1024,4096]{1,0:T(8,128)(2,1)}) %all-gather.4.cloned.1.call-update) | async-done | bytes 8388624 | tf_op jit(solution)/shard_map/all_gather | solution.py:67
  253.2 10.0 %convolution_convert_fusion = bf16[1024,512]{1,0:T(8,128)(2,1)} fusion(bf16[1024,4096]{1,0:T(8,128)(2,1)} %all-gather.4.cloned.1.call-done, bf16[4096,512]{1,0:T(8,128)(2,1)} %param.13), kind=kOutput, calls=%fused_computation.23 | convolution fusion | flops 4295491584 | bytes 13631488 | tf_op jit(solution)/shard_map/dot_general | solution.py:66
  (5 shorter events, 0.1 us)
Async XLA Ops:
  6.5 1.9 copy-start
  6.5 1.6 copy-start.2
  6.5 110.5 %all-gather.6.cloned.1.call-start = ((), (), s32[]{:S(2)}) async-start(), calls=%async_computation.1 | async-start | bytes 17301504 | tf_op jit(solution)/shard_map/all_gather | solution.py:11
  18.1 9.8 %copy-start.3 = (bf16[1024,512]{1,0:T(8,128)(2,1)S(1)}, bf16[1024,512]{1,0:T(8,128)(2,1)}, u32[]{:S(2)}) copy-start(bf16[1024,512]{1,0:T(8,128)(2,1)} %param.10) | copy-start | bytes 3145732
  28.2 4.4 %copy-start.4 = (bf16[2,512,4,128]{3,2,1,0:T(4,128)(2,1)}, bf16[2,512,4,128]{3,2,1,0:T(4,128)(2,1)S(1)}, u32[]{:S(2)}) copy-start(bf16[2,512,4,128]{3,2,1,0:T(4,128)(2,1)S(1)} %reshape.36) | copy-start | bytes 3145732
  32.6 2.5 copy-start.1
  35.1 1.5 copy-start.5
  35.2 218.1 %all-gather.4.cloned.1.call-start = ((), (), s32[]{:S(2)}) async-start(), calls=%async_computation | async-start | bytes 9437184 | tf_op jit(solution)/shard_map/all_gather | solution.py:67
Sparse Core Ops, SparseCore 0:
  35.3 81.7 all-gather.5
  160.0 93.2 all-gather.3
where the time goes:
time: 272 us; the launch traced here: 270 us
  waiting for transfers between devices  168 us (62%)
  other arithmetic  43.8 us (16%)
  matrix products  40 us (15%)
  between operations  13.6 us (5%)
  local copies, waits for them, and re-layouts  4.07 us (1%)
    all_gather x1, waiting for transfers between devices, local(): lax.all_gather(normed, 'head', axis=1, tiled=True)  93.4 us
    all_gather x1, waiting for transfers between devices, carried_in(): pieces = lax.all_gather(value, axis)  74.5 us
    select_n x31, other arithmetic, turn(): return jnp.where(position < mine, longer, subtotal)  37.7 us
    dot_general x2, matrix products, features_of(): jnp.einsum('bthd,hdf->bthf', inputs, frequencies, preferred_element_type=...  19.5 us
    dot_general x1, matrix products, local(): jnp.dot(lax.all_gather(normed, 'head', axis=1, tiled=True), out_weight, p...  10 us
    dot_general x1, matrix products, local(): jnp.einsum('bhts,bshd->bthd', scores, value_spans, preferred_element_type...  5.83 us
  transfers between devices with their start and end apart: 2, of which 2 were waited for; matrix products, arithmetic and copies ran while one was open for 3% of the time, Pallas kernels for 0%

commit v1 on v0

v1 whole, which is shorter than its diff:
```python
import functools
import math

import jax
import jax.numpy as jnp
from jax import lax
from jax.experimental import pallas as pl
from jax.experimental.pallas import tpu as pltpu
from jax.sharding import PartitionSpec as P

MESH = pl.DeviceIdType.MESH
F32 = jnp.float32
BF16 = jnp.bfloat16
HEADS = 4
HDIM = 128
FEATS = 256
ROWS = 1024
BLOCK = 512
TILE = 256
PIECES = 4
RING = 8

TWO_PI_HIGH = 6.28125
TWO_PI_LOW = 2.0 * math.pi - TWO_PI_HIGH
ROUNDER = 12582912.0
SCALE = 1.0 / math.sqrt(128.0)


def half_angle_tables():
    import numpy as np

    root = math.sqrt(2.0 * SCALE)
    nodes = np.cos(np.pi * (np.arange(400) + 0.5) / 400.0) * np.pi**2 * 0.5 + np.pi**2 * 0.5
    angle = np.sqrt(nodes)
    cheb = np.polynomial.chebyshev.Chebyshev
    sine = cheb.fit(nodes, root * np.sin(angle / 2.0) / angle, 4, domain=[0.0, np.pi**2])
    cosine = cheb.fit(nodes, root * np.cos(angle / 2.0), 4, domain=[0.0, np.pi**2])
    poly = np.polynomial.Polynomial
    return (
        [float(v) for v in sine.convert(kind=poly, domain=[-1, 1]).coef],
        [float(v) for v in cosine.convert(kind=poly, domain=[-1, 1]).coef],
    )


SINE, COSINE = half_angle_tables()


def horner(z, table):
    out = z * table[-1] + table[-2]
    for value in table[-3::-1]:
        out = out * z + value
    return out


def cos_sin(phase):
    turns = (phase * (1.0 / (2.0 * math.pi)) + ROUNDER) - ROUNDER
    r = (phase - turns * TWO_PI_HIGH) - turns * TWO_PI_LOW
    z = r * r
    s = r * horner(z, SINE)
    c = horner(z, COSINE)
    return SCALE - s * s, s * c


def dot(a, b, dims=((1,), (0,))):
    return lax.dot_general(a, b, (dims, ((), ())), preferred_element_type=F32)


def columns(h):
    return pl.ds(pl.multiple_of(h * HDIM, HDIM), HDIM)


def tile_rows(p):
    return pl.ds(pl.multiple_of(p * TILE, TILE), TILE)


def kernel(
    q_hbm, k_hbm, v_hbm, freq_ref, gain_ref, w_hbm, out_hbm,
    q_ref, k_ref, v_ref, w_ref, qf, kf, state, local, full, acc, out_ref,
    swap_out, swap_in, first_out, first_in, second_out, second_in, give, take, carry, low,
    load_sem, store_sem, swap_sem, first_sem, second_sem, give_sem, ring_send, ring_recv,
):
    ctx = lax.axis_index("ctx")
    me = lax.axis_index("head")
    core = lax.rem(ctx, 2)
    x = lax.rem(ctx // 2, 4)
    y = ctx // 8
    right, left = lax.rem(me + 1, RING), lax.rem(me + RING - 1, RING)

    def at(y_, x_, core_):
        return (y_ * 4 + x_) * 2 + core_

    def along_x(i):
        return at(y, lax.rem(x + i, 4), core)

    def along_y(i):
        return at(lax.rem(y + i, 4), x, core)

    other = at(y, x, 1 - core)

    loads = [
        pltpu.make_async_copy(src, dst, load_sem.at[i])
        for i, (src, dst) in enumerate(
            ((k_hbm, k_ref), (v_hbm, v_ref), (q_hbm, q_ref), (w_hbm, w_ref))
        )
    ]
    for load in loads:
        load.start()

    barrier = pltpu.get_barrier_semaphore()

    def greet(c_, h_):
        pl.semaphore_signal(
            barrier, inc=1, device_id={"ctx": c_, "head": h_}, device_id_type=MESH
        )

    greet(other, me)
    for i in (1, 2, 3):
        greet(along_x(i), me)
        greet(along_y(i), me)
    greet(ctx, right)
    greet(ctx, left)

    def remote(src, dst, sems, slot, c_):
        return pltpu.make_async_remote_copy(
            src_ref=src, dst_ref=dst, send_sem=sems.at[0, slot], recv_sem=sems.at[1, slot],
            device_id={"ctx": c_, "head": me}, device_id_type=MESH,
        )

    def features(rows_ref, feat_ref, h):
        def chunk(p, _):
            phase = dot(rows_ref[tile_rows(p), columns(h)], freq_ref[h])
            cosine, sine = cos_sin(phase)
            feat_ref[h, tile_rows(p), 0:128] = cosine.astype(BF16)
            feat_ref[h, tile_rows(p), 128:256] = sine.astype(BF16)
            return 0

        lax.fori_loop(0, PIECES, chunk, 0)

    def key_side(j, _):
        h = lax.rem(j + 2 * (1 - core), HEADS)
        features(k_ref, kf, h)
        for b in (0, 1):
            rows = slice(b * BLOCK, (b + 1) * BLOCK)
            state[b, h] = dot(v_ref[rows, columns(h)], kf[h, rows, :], ((0,), (0,)))
        return 0

    loads[0].wait()
    loads[1].wait()
    lax.fori_loop(0, 2, key_side, 0)
    theirs = 2 * (1 - core)
    mine = 2 * core
    for j in (0, 1):
        swap_out[j] = (state[0, theirs + j] + state[1, theirs + j]).astype(BF16)
    pl.semaphore_wait(barrier, 9)
    swap = remote(swap_out, swap_in, swap_sem, 0, other)
    swap.start()
    lax.fori_loop(2, 4, key_side, 0)
    swap.wait()

    def own_total(j):
        return state[0, mine + j] + state[1, mine + j]

    for j in (0, 1):
        first_out[j] = (own_total(j) + swap_in[j].astype(F32)).astype(BF16)
    firsts = []
    for i in (2, 1, 3):
        peer = at(lax.rem(y + core * i, 4), lax.rem(x + (1 - core) * i, 4), core)
        firsts.append(remote(first_out, first_in.at[i - 1], first_sem, i - 1, peer))
        firsts[-1].start()

    loads[2].wait()

    def query_side(h, _):
        features(q_ref, qf, h)
        return 0

    lax.fori_loop(0, HEADS, query_side, 0)

    for copy in firsts:
        copy.wait()
    place = core * y + (1 - core) * x
    for j in (0, 1):
        chip = own_total(j) + swap_in[j].astype(F32)
        before = jnp.zeros_like(chip)
        line = chip
        for i in (1, 2, 3):
            piece = first_in[i - 1, j].astype(F32)
            line = line + piece
            before = before + jnp.where(place >= i, piece, 0.0)
        carry[j] = before
        through = before + chip
        for i in (1, 2, 3):
            column = jnp.where(x + i < 4, through, before)
            second_out[i - 1, j] = jnp.where(core == 0, line, column).astype(BF16)
    seconds = []
    for i in (2, 1, 3):
        peer = at(lax.rem(y + (1 - core) * i, 4), lax.rem(x + core * i, 4), core)
        seconds.append(
            remote(second_out.at[i - 1], second_in.at[i - 1], second_sem, i - 1, peer)
        )
        seconds[-1].start()

    causal = (
        lax.broadcasted_iota(jnp.int32, (TILE, TILE), 0)
        >= lax.broadcasted_iota(jnp.int32, (TILE, TILE), 1)
    )

    def attend(n, _):
        h, b = n // 2, lax.rem(n, 2)
        upper, lower = tile_rows(2 * b), tile_rows(2 * b + 1)

        def scores(rows, cols, masked):
            s = dot(qf[h, rows, :], kf[h, cols, :], ((1,), (1,)))
            return (jnp.where(causal, s, 0.0) if masked else s).astype(BF16)

        v0, v1 = v_ref[upper, columns(h)], v_ref[lower, columns(h)]
        local[upper, columns(h)] = dot(scores(upper, upper, True), v0)
        local[lower, columns(h)] = dot(scores(lower, upper, False), v0) + dot(
            scores(lower, lower, True), v1
        )
        return 0

    lax.fori_loop(0, 6, attend, 0)

    for copy in seconds:
        copy.wait()
    for j in (0, 1):
        total = carry[j]
        for i in (1, 2, 3):
            keep = core + jnp.where(y >= i, 1, 0) > 0
            total = total + jnp.where(keep, second_in[i - 1, j].astype(F32), 0.0)
        give[j] = (total + jnp.where(core == 0, own_total(j), 0.0)).astype(BF16)
        carry[j] = total + jnp.where(core == 1, swap_in[j].astype(F32), 0.0)
    hand = remote(give, take, give_sem, 0, other)
    hand.start()
    lax.fori_loop(6, 8, attend, 0)
    for j in (0, 1):
        low[0, mine + j] = carry[j].astype(BF16)
        low[1, mine + j] = (carry[j] + state[0, mine + j]).astype(BF16)
    hand.wait()
    for j in (0, 1):
        arrived = take[j].astype(F32)
        low[0, theirs + j] = arrived.astype(BF16)
        low[1, theirs + j] = (arrived + state[0, theirs + j]).astype(BF16)

    def hop(d, k, p):
        slot = lax.rem(me + RING - (k - 1), RING) if d == 0 else lax.rem(me + (k - 1), RING)
        piece = full.at[slot, tile_rows(p), :]
        return pltpu.make_async_remote_copy(
            src_ref=piece, dst_ref=piece,
            send_sem=ring_send.at[d, k - 1, p], recv_sem=ring_recv.at[d, k - 1, p],
            device_id={"ctx": ctx, "head": right if d == 0 else left}, device_id_type=MESH,
        )

    def project(slot, p, first=False):
        term = dot(
            full[slot, tile_rows(p), :], w_ref[pl.ds(pl.multiple_of(slot * 512, 512), 512), :]
        )
        if first:
            acc[tile_rows(p), :] = term
        else:
            acc[tile_rows(p), :] += term

    def finish(p, _):
        rows = tile_rows(p)
        for h in range(HEADS):
            cols = slice(h * HDIM, (h + 1) * HDIM)
            attended = local[rows, cols] + dot(
                qf[h, rows, :], low[p // 2, h], ((1,), (1,))
            )
            square = jnp.mean(attended * attended, axis=-1, keepdims=True)
            gain = gain_ref[0:1, cols].astype(F32)
            full[me, rows, cols] = (attended * lax.rsqrt(square + 1e-06) * gain).astype(BF16)
        hop(0, 1, p).start()
        hop(1, 1, p).start()
        return 0

    lax.fori_loop(0, PIECES, finish, 0)
    loads[3].wait()

    def own(p, _):
        project(me, p, True)
        return 0

    lax.fori_loop(0, PIECES, own, 0)

    def receive(n, _):
        k, p = n // PIECES + 1, lax.rem(n, PIECES)
        for d in (0, 1):
            hop(d, k, p).wait_recv()
            further = (k < 3) | ((p < 2) if d == 0 else (p >= 2))

            @pl.when(further)
            def _():
                hop(d, k + 1, p).start()

            slot = lax.rem(me + RING - k, RING) if d == 0 else lax.rem(me + k, RING)
            project(slot, p)
        return 0

    lax.fori_loop(0, 3 * PIECES, receive, 0)

    opposite = lax.rem(me + 4, RING)
    stores = []
    for p, d in ((0, 0), (2, 1), (1, 0), (3, 1)):
        hop(d, 4, p).wait_recv()
        project(opposite, p)
        out_ref[tile_rows(p), :] = acc[tile_rows(p), :].astype(BF16)
        stores.append(
            pltpu.make_async_copy(
                out_ref.at[tile_rows(p), :], out_hbm.at[tile_rows(p), :], store_sem.at[p]
            )
        )
        stores[-1].start()

    def drain(n, _):
        k, p = n // PIECES + 1, lax.rem(n, PIECES)
        for d in (0, 1):
            hop(d, k, p).wait_send()
        return 0

    lax.fori_loop(0, 3 * PIECES, drain, 0)
    for p, d in ((0, 0), (2, 1), (1, 0), (3, 1)):
        hop(d, 4, p).wait_send()
    for store in stores:
        store.wait()


def local(query_rows, key_rows, value_rows, frequencies, norm_gain, out_weight):
    anywhere = pl.BlockSpec(memory_space=pl.ANY)
    vmem = pl.BlockSpec(memory_space=pltpu.VMEM)
    pair = (2, HDIM, FEATS)
    return pl.pallas_call(
        kernel,
        out_shape=jax.ShapeDtypeStruct((ROWS, 512), BF16),
        in_specs=[anywhere, anywhere, anywhere, vmem, vmem, anywhere],
        out_specs=anywhere,
        scratch_shapes=[
            pltpu.VMEM((ROWS, 512), BF16),
            pltpu.VMEM((ROWS, 512), BF16),
            pltpu.VMEM((ROWS, 512), BF16),
            pltpu.VMEM((4096, 512), BF16),
            pltpu.VMEM((HEADS, ROWS, FEATS), BF16),
            pltpu.VMEM((HEADS, ROWS, FEATS), BF16),
            pltpu.VMEM((2, HEADS, HDIM, FEATS), F32),
            pltpu.VMEM((ROWS, 512), F32),
            pltpu.VMEM((RING, ROWS, 512), BF16),
            pltpu.VMEM((ROWS, 512), F32),
            pltpu.VMEM((ROWS, 512), BF16),
            pltpu.VMEM(pair, BF16),
            pltpu.VMEM(pair, BF16),
            pltpu.VMEM(pair, BF16),
            pltpu.VMEM((3,) + pair, BF16),
            pltpu.VMEM((3,) + pair, BF16),
            pltpu.VMEM((3,) + pair, BF16),
            pltpu.VMEM(pair, BF16),
            pltpu.VMEM(pair, BF16),
            pltpu.VMEM(pair, F32),
            pltpu.VMEM((2, HEADS, HDIM, FEATS), BF16),
            pltpu.SemaphoreType.DMA((4,)),
            pltpu.SemaphoreType.DMA((PIECES,)),
            pltpu.SemaphoreType.DMA((2, 1)),
            pltpu.SemaphoreType.DMA((2, 3)),
            pltpu.SemaphoreType.DMA((2, 3)),
            pltpu.SemaphoreType.DMA((2, 1)),
            pltpu.SemaphoreType.DMA((2, 4, PIECES)),
            pltpu.SemaphoreType.DMA((2, 4, PIECES)),
        ],
        compiler_params=pltpu.CompilerParams(
            collective_id=0, has_side_effects=True, vmem_limit_bytes=50 * 2**20
        ),
        cost_estimate=pl.CostEstimate(
            flops=7 * 10**9, bytes_accessed=9 * 2**20, transcendentals=0
        ),
    )(query_rows, key_rows, value_rows, frequencies, norm_gain.reshape(1, 512), out_weight)


def solution(mesh):
    return jax.shard_map(
        local,
        mesh=mesh,
        in_specs=(
            P("ctx", "head"),
            P("ctx", "head"),
            P("ctx", "head"),
            P("head", None, None),
            P("head"),
            P(None, "head"),
        ),
        out_specs=P("ctx", "head"),
        check_vma=False,
    )
```

time: 272 us -> 116 us (0.43)
  waiting for transfers between devices: 168 us -> 0 us
  Pallas kernels: 0 us -> 111 us
  other arithmetic: 43.8 us -> 0 us
  matrix products: 40 us -> 0 us
  between operations: 13.6 us -> 0.01 us
    all_gather x2 -> x0, waiting for transfers between devices: 168 us -> none  [the longest x1 93.4 us: local(): lax.all_gather(normed, 'head', axis=1, tiled=True)]
    pallas_call x0 -> x1, Pallas kernels: none -> 111 us  [local(): pl.pallas_call(kernel, out_shape=jax.ShapeDtypeStruct((ROWS, 512), BF16),...]
    dot_general x6 -> x0, matrix products: 40 us -> none  [the longest x2 19.5 us: features_of(): jnp.einsum('bthd,hdf->bthf', inputs, frequencies, preferred_element_type=...]
    select_n x31 -> x0, other arithmetic: 37.7 us -> none  [turn(): return jnp.where(position < mine, longer, subtotal)]
    convert_element_type x2 -> x0, other arithmetic: 4.68 us -> none  [the longest x1 4.4 us: features_of(): return (joined * (1.0 / math.sqrt(freq_count))).astype(jnp.bfloat16)]
    unnamed x13 -> x7, local copies, waits for them, and re-layouts: 1.3 us -> 4.32 us
  transfers between devices with their start and end apart: 2 -> 0, of which waited for: 2 -> 0; matrix products, arithmetic and copies ran while one was open for 3% -> 0% of each run, Pallas kernels for 0% -> 0%
where the time goes in v1:
time: 116 us
  Pallas kernels  111 us (96%)
  local copies, waits for them, and re-layouts  5.01 us (4%)
    pallas_call x1, Pallas kernels, local(): pl.pallas_call(kernel, out_shape=jax.ShapeDtypeStruct((ROWS, 512), BF16),...  111 us
    unnamed x7, local copies, waits for them, and re-layouts  4.32 us

profile of v1, /device:TPU:1, one launch (start us, length us, event | category | flops | bytes accessed | tf_op | source)
XLA Modules:
  0.0 115.9 jit_solution(1508773410178400059)
XLA Ops:
  0.0 0.7 reshape.3.gain_ref
  0.7 0.0 copy-start
  0.7 1.2 %copy-done = bf16[1024,512]{1,0:T(8,128)(2,1)S(1)} copy-done((bf16[1024,512]{1,0:T(8,128)(2,1)S(1)}, bf16[1024,512]{1,0:T(8,128)(2,1)}, u32[]{:S(2)}) %copy-start) | copy-done | bytes 1048600
  1.9 0.0 copy-start.1
  1.9 1.2 %copy-done.1 = bf16[1024,512]{1,0:T(8,128)(2,1)S(1)} copy-done((bf16[1024,512]{1,0:T(8,128)(2,1)S(1)}, bf16[1024,512]{1,0:T(8,128)(2,1)}, u32[]{:S(2)}) %copy-start.1) | copy-done | bytes 1048600
  3.1 0.0 copy-start.2
  3.1 0.9 copy-done.2
  4.0 110.9 %shard_map.64 = bf16[1024,512]{1,0:T(8,128)(2,1)S(1)} custom-call(bf16[1024,512]{1,0:T(8,128)(2,1)S(1)} %copy-done, bf16[1024,512]{1,0:T(8,128)(2,1)S(1)} %copy-done.1, bf16[1024,512]{1,0:T(8,128)(2,1)} %v_hbm.1, bf16[4,128,128]{2,1,0:T(8,128)(2,1)S(1)} %copy-done.2, bf16[1,512]{1,0:T(2,128)(2,1)S(1)} %reshape.3.gain_ref, bf16[4096,512]{1,0:T(8,128)(2,1)} %w_hbm.1), custom_call_target="tpu_custom_call" | custom-call | flops 7000000000 | bytes 9437184 | tf_op jit(solution)/shard_map/pallas_call | solution.py:333
  114.9 1.0 copy.8
Async XLA Ops:
  0.7 1.2 %copy-start = (bf16[1024,512]{1,0:T(8,128)(2,1)S(1)}, bf16[1024,512]{1,0:T(8,128)(2,1)}, u32[]{:S(2)}) copy-start(bf16[1024,512]{1,0:T(8,128)(2,1)} %q_hbm.1) | copy-start | bytes 3145732
  1.9 1.2 %copy-start.1 = (bf16[1024,512]{1,0:T(8,128)(2,1)S(1)}, bf16[1024,512]{1,0:T(8,128)(2,1)}, u32[]{:S(2)}) copy-start(bf16[1024,512]{1,0:T(8,128)(2,1)} %k_hbm.1) | copy-start | bytes 3145732
  3.1 0.9 copy-start.2

commit v2 on v1

--- a/solution.py
+++ b/solution.py
@@ -19,6 +19,7 @@
 TILE = 256
 PIECES = 4
 RING = 8
+SLICE = 128
 
 TWO_PI_HIGH = 6.28125
 TWO_PI_LOW = 2.0 * math.pi - TWO_PI_HIGH
@@ -75,16 +76,22 @@
 
 def kernel(
     q_hbm, k_hbm, v_hbm, freq_ref, gain_ref, w_hbm, out_hbm,
-    q_ref, k_ref, v_ref, w_ref, qf, kf, state, local, full, acc, out_ref,
+    q_ref, k_ref, v_ref, w_ref, qf, kf, state, local, normed, full, acc, out_ref,
     swap_out, swap_in, first_out, first_in, second_out, second_in, give, take, carry, low,
-    load_sem, store_sem, swap_sem, first_sem, second_sem, give_sem, ring_send, ring_recv,
+    load_sem, swap_sem, first_sem, second_sem, give_sem,
+    w_z_sem, w_first_sem, w_second_sem, w_core_sem, rows_sem, pass_sem, back_sem,
 ):
     ctx = lax.axis_index("ctx")
     me = lax.axis_index("head")
     core = lax.rem(ctx, 2)
     x = lax.rem(ctx // 2, 4)
     y = ctx // 8
-    right, left = lax.rem(me + 1, RING), lax.rem(me + RING - 1, RING)
+    pair = me // 2
+    sign = 1 - 2 * lax.rem(me, 2)
+    mate = lax.rem(me + sign + RING, RING)
+
+    def member(r):
+        return 2 * r + lax.rem(me + pair // 2 + r // 2, 2)
 
     def at(y_, x_, core_):
         return (y_ * 4 + x_) * 2 + core_
@@ -100,7 +107,7 @@
     loads = [
         pltpu.make_async_copy(src, dst, load_sem.at[i])
         for i, (src, dst) in enumerate(
-            ((k_hbm, k_ref), (v_hbm, v_ref), (q_hbm, q_ref), (w_hbm, w_ref))
+            ((k_hbm, k_ref), (v_hbm, v_ref), (q_hbm, q_ref), (w_hbm, w_ref.at[pair]))
         )
     ]
     for load in loads:
@@ -117,14 +124,73 @@
     for i in (1, 2, 3):
         greet(along_x(i), me)
         greet(along_y(i), me)
-    greet(ctx, right)
-    greet(ctx, left)
+    for i in (1, 2, 3, 5, 6, 7):
+        greet(ctx, lax.rem(me + i, RING))
 
     def remote(src, dst, sems, slot, c_):
         return pltpu.make_async_remote_copy(
             src_ref=src, dst_ref=dst, send_sem=sems.at[0, slot], recv_sem=sems.at[1, slot],
             device_id={"ctx": c_, "head": me}, device_id_type=MESH,
         )
+
+    def remote_z(src, dst, sems, slot, h_):
+        return pltpu.make_async_remote_copy(
+            src_ref=src, dst_ref=dst, send_sem=sems.at[0, slot], recv_sem=sems.at[1, slot],
+            device_id={"ctx": ctx, "head": h_}, device_id_type=MESH,
+        )
+
+    def first_peer(i):
+        return at(lax.rem(y + core * i, 4), lax.rem(x + (1 - core) * i, 4), core)
+
+    def second_peer(i):
+        return at(lax.rem(y + (1 - core) * i, 4), lax.rem(x + core * i, 4), core)
+
+    first_place = core * y + (1 - core) * x
+    second_place = core * x + (1 - core) * y
+    half_rows = core * 2048
+
+    def slot_of(i):
+        return lax.rem(pair + 4 - i, 4)
+
+    def w_piece(i, start, size):
+        return w_ref.at[slot_of(i), pl.ds(pl.multiple_of(start, SLICE), size), :]
+
+    line_start = half_rows + second_place * 512
+    slice_start = line_start + first_place * SLICE
+
+    def w_z(i):
+        rows = pl.ds(pl.multiple_of(slice_start, SLICE), SLICE)
+        return remote_z(
+            w_hbm.at[rows, :], w_ref.at[pair, rows, :], w_z_sem, i - 1, member(lax.rem(pair + i, 4))
+        )
+
+    def w_z_arrived(i):
+        piece = w_piece(i, slice_start, SLICE)
+        remote_z(piece, piece, w_z_sem, i - 1, member(slot_of(i))).wait_recv()
+
+    def w_first(i, o):
+        piece = w_piece(i, slice_start, SLICE)
+        return remote(piece, piece, w_first_sem.at[i - 1], o - 1, first_peer(o))
+
+    def w_first_arrived(i, o):
+        piece = w_piece(i, line_start + lax.rem(first_place + 4 - o, 4) * SLICE, SLICE)
+        remote(piece, piece, w_first_sem.at[i - 1], o - 1, first_peer(o)).wait_recv()
+
+    def w_second(i, o):
+        piece = w_piece(i, line_start, 512)
+        return remote(piece, piece, w_second_sem.at[i - 1], o - 1, second_peer(o))
+
+    def w_second_arrived(i, o):
+        piece = w_piece(i, half_rows + lax.rem(second_place + 4 - o, 4) * 512, 512)
+        remote(piece, piece, w_second_sem.at[i - 1], o - 1, second_peer(o)).wait_recv()
+
+    def w_core(i):
+        piece = w_piece(i, half_rows, 2048)
+        return remote(piece, piece, w_core_sem, i - 1, other)
+
+    def w_core_arrived(i):
+        piece = w_piece(i, 2048 - half_rows, 2048)
+        remote(piece, piece, w_core_sem, i - 1, other).wait_recv()
 
     def features(rows_ref, feat_ref, h):
         def chunk(p, _):
@@ -151,9 +217,11 @@
     mine = 2 * core
     for j in (0, 1):
         swap_out[j] = (state[0, theirs + j] + state[1, theirs + j]).astype(BF16)
-    pl.semaphore_wait(barrier, 9)
+    pl.semaphore_wait(barrier, 13)
     swap = remote(swap_out, swap_in, swap_sem, 0, other)
     swap.start()
+    for i in (1, 2, 3):
+        w_z(i).start()
     lax.fori_loop(2, 4, key_side, 0)
     swap.wait()
 
@@ -164,8 +232,9 @@
         first_out[j] = (own_total(j) + swap_in[j].astype(F32)).astype(BF16)
     firsts = []
     for i in (2, 1, 3):
-        peer = at(lax.rem(y + core * i, 4), lax.rem(x + (1 - core) * i, 4), core)
-        firsts.append(remote(first_out, first_in.at[i - 1], first_sem, i - 1, peer))
+        firsts.append(
+            remote(first_out, first_in.at[i - 1], first_sem, i - 1, first_peer(i))
+        )
         firsts[-1].start()
 
     loads[2].wait()
@@ -178,7 +247,6 @@
 
     for copy in firsts:
         copy.wait()
-    place = core * y + (1 - core) * x
     for j in (0, 1):
         chip = own_total(j) + swap_in[j].astype(F32)
         before = jnp.zeros_like(chip)
@@ -186,7 +254,7 @@
         for i in (1, 2, 3):
             piece = first_in[i - 1, j].astype(F32)
             line = line + piece
-            before = before + jnp.where(place >= i, piece, 0.0)
+            before = before + jnp.where(first_place >= i, piece, 0.0)
         carry[j] = before
         through = before + chip
         for i in (1, 2, 3):
@@ -194,11 +262,14 @@
             second_out[i - 1, j] = jnp.where(core == 0, line, column).astype(BF16)
     seconds = []
     for i in (2, 1, 3):
-        peer = at(lax.rem(y + (1 - core) * i, 4), lax.rem(x + core * i, 4), core)
         seconds.append(
-            remote(second_out.at[i - 1], second_in.at[i - 1], second_sem, i - 1, peer)
+            remote(second_out.at[i - 1], second_in.at[i - 1], second_sem, i - 1, second_peer(i))
         )
         seconds[-1].start()
+    for i in (1, 2, 3):
+        w_z_arrived(i)
+        for o in (2, 1, 3):
+            w_first(i, o).start()
 
     causal = (
         lax.broadcasted_iota(jnp.int32, (TILE, TILE), 0)
@@ -243,87 +314,112 @@
         low[0, theirs + j] = arrived.astype(BF16)
         low[1, theirs + j] = (arrived + state[0, theirs + j]).astype(BF16)
 
-    def hop(d, k, p):
-        slot = lax.rem(me + RING - (k - 1), RING) if d == 0 else lax.rem(me + (k - 1), RING)
-        piece = full.at[slot, tile_rows(p), :]
-        return pltpu.make_async_remote_copy(
-            src_ref=piece, dst_ref=piece,
-            send_sem=ring_send.at[d, k - 1, p], recv_sem=ring_recv.at[d, k - 1, p],
-            device_id={"ctx": ctx, "head": right if d == 0 else left}, device_id_type=MESH,
-        )
-
-    def project(slot, p, first=False):
-        term = dot(
-            full[slot, tile_rows(p), :], w_ref[pl.ds(pl.multiple_of(slot * 512, 512), 512), :]
-        )
-        if first:
-            acc[tile_rows(p), :] = term
-        else:
-            acc[tile_rows(p), :] += term
-
-    def finish(p, _):
-        rows = tile_rows(p)
+    def to_pair(k):
+        target = mate if k == 0 else lax.rem(me + sign * {1: -1, 2: 2, 3: -3}[k] + RING, RING)
+        piece = normed.at[tile_rows(target // 2), :]
+        return remote_z(piece, full.at[me], rows_sem, k, target)
+
+    def rows_arrived(k):
+        slot = mate if k == 0 else lax.rem(me - sign * k + RING, RING)
+        piece = full.at[slot]
+        remote_z(piece, piece, rows_sem, k, slot).wait_recv()
+
+    def pass_on(k):
+        piece = full.at[lax.rem(me - sign * k + RING, RING)]
+        return remote_z(piece, piece, pass_sem, k - 1, mate)
+
+    def passed(k):
+        piece = full.at[lax.rem(me + sign * (k + 1) + RING, RING)]
+        remote_z(piece, piece, pass_sem, k - 1, mate).wait_recv()
+
+    def finish(q):
+        rows = tile_rows(q)
         for h in range(HEADS):
             cols = slice(h * HDIM, (h + 1) * HDIM)
             attended = local[rows, cols] + dot(
-                qf[h, rows, :], low[p // 2, h], ((1,), (1,))
+                qf[h, rows, :], low[q // 2, h], ((1,), (1,))
             )
             square = jnp.mean(attended * attended, axis=-1, keepdims=True)
             gain = gain_ref[0:1, cols].astype(F32)
-            full[me, rows, cols] = (attended * lax.rsqrt(square + 1e-06) * gain).astype(BF16)
-        hop(0, 1, p).start()
-        hop(1, 1, p).start()
-        return 0
-
-    lax.fori_loop(0, PIECES, finish, 0)
+            normed[rows, cols] = (attended * lax.rsqrt(square + 1e-06) * gain).astype(BF16)
+
+    for k, step in ((3, 2), (2, sign), (1, -sign), (0, 0)):
+        finish(lax.rem(pair + step + 4, 4))
+        to_pair(k).start()
+    full[me] = normed[tile_rows(pair), :]
+
+    def line(i):
+        for o in (1, 2, 3):
+            w_first_arrived(i, o)
+        for o in (2, 1, 3):
+            w_second(i, o).start()
+
+    def halves(i):
+        for o in (1, 2, 3):
+            w_second_arrived(i, o)
+        w_core(i).start()
+
+    line(1)
+    for k in (1, 2):
+        rows_arrived(k)
+        pass_on(k).start()
+    halves(1)
+    line(2)
+    rows_arrived(3)
+    pass_on(3).start()
+    halves(2)
+    line(3)
+    rows_arrived(0)
+    for k in (1, 2, 3):
+        passed(k)
+
+    def project(slot, target):
+        for s in (0, 2, 4, 6):
+            term = dot(full[s], w_ref[slot, s * 512 : s * 512 + 512, :]) + dot(
+                full[s + 1], w_ref[slot, s * 512 + 512 : s * 512 + 1024, :]
+            )
+            if s == 0:
+                acc[...] = term
+            elif s < 6:
+                acc[...] += term
+            else:
+                out_ref[target] = (acc[...] + term).astype(BF16)
+
+    def back(i):
+        return remote_z(
+            out_ref.at[i], out_hbm.at[tile_rows(pair), :], back_sem, i - 1, member(slot_of(i))
+        )
+
+    def back_arrived(i):
+        r = lax.rem(pair + i, 4)
+        remote_z(out_ref.at[i], out_hbm.at[tile_rows(r), :], back_sem, i - 1, member(r)).wait_recv()
+
+    for i in (1, 2):
+        w_core_arrived(i)
+        project(slot_of(i), i)
+        back(i).start()
     loads[3].wait()
-
-    def own(p, _):
-        project(me, p, True)
-        return 0
-
-    lax.fori_loop(0, PIECES, own, 0)
-
-    def receive(n, _):
-        k, p = n // PIECES + 1, lax.rem(n, PIECES)
-        for d in (0, 1):
-            hop(d, k, p).wait_recv()
-            further = (k < 3) | ((p < 2) if d == 0 else (p >= 2))
-
-            @pl.when(further)
-            def _():
-                hop(d, k + 1, p).start()
-
-            slot = lax.rem(me + RING - k, RING) if d == 0 else lax.rem(me + k, RING)
-            project(slot, p)
-        return 0
-
-    lax.fori_loop(0, 3 * PIECES, receive, 0)
-
-    opposite = lax.rem(me + 4, RING)
-    stores = []
-    for p, d in ((0, 0), (2, 1), (1, 0), (3, 1)):
-        hop(d, 4, p).wait_recv()
-        project(opposite, p)
-        out_ref[tile_rows(p), :] = acc[tile_rows(p), :].astype(BF16)
-        stores.append(
-            pltpu.make_async_copy(
-                out_ref.at[tile_rows(p), :], out_hbm.at[tile_rows(p), :], store_sem.at[p]
-            )
-        )
-        stores[-1].start()
-
-    def drain(n, _):
-        k, p = n // PIECES + 1, lax.rem(n, PIECES)
-        for d in (0, 1):
-            hop(d, k, p).wait_send()
-        return 0
-
-    lax.fori_loop(0, 3 * PIECES, drain, 0)
-    for p, d in ((0, 0), (2, 1), (1, 0), (3, 1)):
-        hop(d, 4, p).wait_send()
-    for store in stores:
-        store.wait()
+    project(pair, 0)
+    keep = pltpu.make_async_copy(out_ref.at[0], out_hbm.at[tile_rows(pair), :], load_sem.at[0])
+    keep.start()
+    halves(3)
+    w_core_arrived(3)
+    project(slot_of(3), 3)
+    back(3).start()
+
+    keep.wait()
+    for i in (1, 2, 3):
+        w_z(i).wait_send()
+        w_core(i).wait_send()
+        pass_on(i).wait_send()
+        for o in (1, 2, 3):
+            w_first(i, o).wait_send()
+            w_second(i, o).wait_send()
+    for k in (0, 1, 2, 3):
+        to_pair(k).wait_send()
+    for i in (1, 2, 3):
+        back(i).wait_send()
+        back_arrived(i)
 
 
 def local(query_rows, key_rows, value_rows, frequencies, norm_gain, out_weight):
@@ -339,14 +435,15 @@
             pltpu.VMEM((ROWS, 512), BF16),
             pltpu.VMEM((ROWS, 512), BF16),
             pltpu.VMEM((ROWS, 512), BF16),
-            pltpu.VMEM((4096, 512), BF16),
+            pltpu.VMEM((4, 4096, 512), BF16),
             pltpu.VMEM((HEADS, ROWS, FEATS), BF16),
             pltpu.VMEM((HEADS, ROWS, FEATS), BF16),
             pltpu.VMEM((2, HEADS, HDIM, FEATS), F32),
             pltpu.VMEM((ROWS, 512), F32),
-            pltpu.VMEM((RING, ROWS, 512), BF16),
-            pltpu.VMEM((ROWS, 512), F32),
             pltpu.VMEM((ROWS, 512), BF16),
+            pltpu.VMEM((RING, TILE, 512), BF16),
+            pltpu.VMEM((TILE, 512), F32),
+            pltpu.VMEM((4, TILE, 512), BF16),
             pltpu.VMEM(pair, BF16),
             pltpu.VMEM(pair, BF16),
             pltpu.VMEM(pair, BF16),
@@ -358,16 +455,20 @@
             pltpu.VMEM(pair, F32),
             pltpu.VMEM((2, HEADS, HDIM, FEATS), BF16),
             pltpu.SemaphoreType.DMA((4,)),
-            pltpu.SemaphoreType.DMA((PIECES,)),
             pltpu.SemaphoreType.DMA((2, 1)),
             pltpu.SemaphoreType.DMA((2, 3)),
             pltpu.SemaphoreType.DMA((2, 3)),
             pltpu.SemaphoreType.DMA((2, 1)),
-            pltpu.SemaphoreType.DMA((2, 4, PIECES)),
-            pltpu.SemaphoreType.DMA((2, 4, PIECES)),
+            pltpu.SemaphoreType.DMA((2, 3)),
+            pltpu.SemaphoreType.DMA((3, 2, 3)),
+            pltpu.SemaphoreType.DMA((3, 2, 3)),
+            pltpu.SemaphoreType.DMA((2, 3)),
+            pltpu.SemaphoreType.DMA((2, 4)),
+            pltpu.SemaphoreType.DMA((2, 3)),
+            pltpu.SemaphoreType.DMA((2, 3)),
         ],
         compiler_params=pltpu.CompilerParams(
-            collective_id=0, has_side_effects=True, vmem_limit_bytes=50 * 2**20
+            collective_id=0, has_side_effects=True, vmem_limit_bytes=63 * 2**20
         ),
         cost_estimate=pl.CostEstimate(
             flops=7 * 10**9, bytes_accessed=9 * 2**20, transcendentals=0

time: 116 us -> 106 us (0.914)
  the two profiles are of different devices: /device:TPU:1 before, /device:TPU:33 now
where the time goes in v2:
time: 106 us
  Pallas kernels  102 us (96%)
  local copies, waits for them, and re-layouts  3.52 us (3%)
    pallas_call x1, Pallas kernels, local(): pl.pallas_call(kernel, out_shape=jax.ShapeDtypeStruct((ROWS, 512), BF16),...  102 us
    unnamed x1, local copies, waits for them, and re-layouts  2.26 us

profile of v2, /device:TPU:33, one launch (start us, length us, event | category | flops | bytes accessed | tf_op | source)
XLA Modules:
  0.0 106.0 jit_solution(16562714228491726295)
XLA Ops:
  0.0 1.3 %reshape.3.gain_ref = bf16[1,512]{1,0:T(2,128)(2,1)} reshape(bf16[512]{0:T(512)(128)(2,1)} %param.10) | data formatting | bytes 2048 | tf_op jit(solution)/shard_map/reshape | solution.py:476
  1.3 102.5 %shard_map.64 = bf16[1024,512]{1,0:T(8,128)(2,1)} custom-call(bf16[1024,512]{1,0:T(8,128)(2,1)} %q_hbm.1, bf16[1024,512]{1,0:T(8,128)(2,1)} %k_hbm.1, bf16[1024,512]{1,0:T(8,128)(2,1)} %v_hbm.1, bf16[4,128,128]{2,1,0:T(8,128)(2,1)} %freq_ref.1, bf16[1,512]{1,0:T(2,128)(2,1)} %reshape.3.gain_ref, bf16[4096,512]{1,0:T(8,128)(2,1)} %w_hbm.1), custom_call_target="tpu_custom_call" | custom-call | flops 7000000000 | bytes 9437184 | tf_op jit(solution)/shard_map/pallas_call | solution.py:429
  103.7 2.3 %copy.8 = bf16[1024,512]{1,0:T(8,128)(2,1)} copy(bf16[1024,512]{1,0:T(8,128)(2,1)} %shard_map.64) | data formatting | bytes 2097152

commit v3 on v2

v3 whole, which is shorter than its diff:
```python
import functools
import math

import jax
import jax.numpy as jnp
from jax import lax
from jax.experimental import pallas as pl
from jax.experimental.pallas import tpu as pltpu
from jax.sharding import PartitionSpec as P

MESH = pl.DeviceIdType.MESH
F32 = jnp.float32
BF16 = jnp.bfloat16
HEADS = 4
HDIM = 128
FEATS = 256
ROWS = 1024
BLOCK = 512
TILE = 256
PIECES = 4
RING = 8
SLICE = 128
SEATS = 8
PART = 64
HALF = 128

TWO_PI_HIGH = 6.28125
TWO_PI_LOW = 2.0 * math.pi - TWO_PI_HIGH
ROUNDER = 12582912.0
SCALE = 1.0 / math.sqrt(128.0)


def half_angle_tables():
    import numpy as np

    root = math.sqrt(2.0 * SCALE)
    nodes = np.cos(np.pi * (np.arange(400) + 0.5) / 400.0) * np.pi**2 * 0.5 + np.pi**2 * 0.5
    angle = np.sqrt(nodes)
    cheb = np.polynomial.chebyshev.Chebyshev
    sine = cheb.fit(nodes, root * np.sin(angle / 2.0) / angle, 4, domain=[0.0, np.pi**2])
    cosine = cheb.fit(nodes, root * np.cos(angle / 2.0), 4, domain=[0.0, np.pi**2])
    poly = np.polynomial.Polynomial
    return (
        [float(v) for v in sine.convert(kind=poly, domain=[-1, 1]).coef],
        [float(v) for v in cosine.convert(kind=poly, domain=[-1, 1]).coef],
    )


SINE, COSINE = half_angle_tables()


def horner(z, table):
    out = z * table[-1] + table[-2]
    for value in table[-3::-1]:
        out = out * z + value
    return out


def cos_sin(phase):
    turns = (phase * (1.0 / (2.0 * math.pi)) + ROUNDER) - ROUNDER
    r = (phase - turns * TWO_PI_HIGH) - turns * TWO_PI_LOW
    z = r * r
    s = r * horner(z, SINE)
    c = horner(z, COSINE)
    return SCALE - s * s, s * c


def dot(a, b, dims=((1,), (0,))):
    return lax.dot_general(a, b, (dims, ((), ())), preferred_element_type=F32)


def columns(h):
    return pl.ds(pl.multiple_of(h * HDIM, HDIM), HDIM)


def tile_rows(p):
    return pl.ds(pl.multiple_of(p * TILE, TILE), TILE)


def kernel(
    q_hbm, k_hbm, v_hbm, freq_hbm, gain_hbm, w_hbm, out_hbm,
    q_ref, k_ref, v_ref, freq_ref, gain_ref, w_ref, qf, kf, state, local, normed, full, acc, out_ref,
    total, parts, row_out, row_in, sums, low,
    load_sem, parts_sem, row_sem, sums_sem,
    w_z_sem, w_first_sem, w_second_sem, w_core_sem, rows_sem, pass_sem, back_sem,
):
    ctx = lax.axis_index("ctx")
    me = lax.axis_index("head")
    core = lax.rem(ctx, 2)
    x = lax.rem(ctx // 2, 4)
    y = ctx // 8
    pair = me // 2
    sign = 1 - 2 * lax.rem(me, 2)
    mate = lax.rem(me + sign + RING, RING)

    def member(r):
        return 2 * r + lax.rem(me + pair // 2 + r // 2, 2)

    def at(y_, x_, core_):
        return (y_ * 4 + x_) * 2 + core_

    def row_seat(i):
        return y * SEATS + lax.rem(i, SEATS)

    def along_y(i):
        return at(lax.rem(y + i, 4), x, core)

    other = at(y, x, 1 - core)
    seat = 2 * x + core

    loads = [
        pltpu.make_async_copy(src, dst, load_sem.at[i])
        for i, (src, dst) in enumerate(
            (
                (freq_hbm, freq_ref), (k_hbm, k_ref), (v_hbm, v_ref), (q_hbm, q_ref),
                (gain_hbm, gain_ref), (w_hbm, w_ref.at[pair]),
            )
        )
    ]
    for load in loads:
        load.start()

    barrier = pltpu.get_barrier_semaphore()

    def greet(c_, h_):
        pl.semaphore_signal(
            barrier, inc=1, device_id={"ctx": c_, "head": h_}, device_id_type=MESH
        )

    for i in range(1, SEATS):
        greet(row_seat(seat + i), me)
    for i in (1, 2, 3):
        greet(along_y(i), me)
    for i in (1, 2, 3, 5, 6, 7):
        greet(ctx, lax.rem(me + i, RING))

    def remote(src, dst, sems, slot, c_):
        return pltpu.make_async_remote_copy(
            src_ref=src, dst_ref=dst, send_sem=sems.at[0, slot], recv_sem=sems.at[1, slot],
            device_id={"ctx": c_, "head": me}, device_id_type=MESH,
        )

    def remote_z(src, dst, sems, slot, h_):
        return pltpu.make_async_remote_copy(
            src_ref=src, dst_ref=dst, send_sem=sems.at[0, slot], recv_sem=sems.at[1, slot],
            device_id={"ctx": ctx, "head": h_}, device_id_type=MESH,
        )

    def first_peer(i):
        return at(lax.rem(y + core * i, 4), lax.rem(x + (1 - core) * i, 4), core)

    def second_peer(i):
        return at(lax.rem(y + (1 - core) * i, 4), lax.rem(x + core * i, 4), core)

    first_place = core * y + (1 - core) * x
    second_place = core * x + (1 - core) * y
    half_rows = core * 2048

    def slot_of(i):
        return lax.rem(pair + 4 - i, 4)

    def w_piece(i, start, size):
        return w_ref.at[slot_of(i), pl.ds(pl.multiple_of(start, SLICE), size), :]

    line_start = half_rows + second_place * 512
    slice_start = line_start + first_place * SLICE

    def w_z(i):
        rows = pl.ds(pl.multiple_of(slice_start, SLICE), SLICE)
        return remote_z(
            w_hbm.at[rows, :], w_ref.at[pair, rows, :], w_z_sem, i - 1, member(lax.rem(pair + i, 4))
        )

    def w_z_arrived(i):
        piece = w_piece(i, slice_start, SLICE)
        remote_z(piece, piece, w_z_sem, i - 1, member(slot_of(i))).wait_recv()

    def w_first(i, o):
        piece = w_piece(i, slice_start, SLICE)
        return remote(piece, piece, w_first_sem.at[i - 1], o - 1, first_peer(o))

    def w_first_arrived(i, o):
        piece = w_piece(i, line_start + lax.rem(first_place + 4 - o, 4) * SLICE, SLICE)
        remote(piece, piece, w_first_sem.at[i - 1], o - 1, first_peer(o)).wait_recv()

    def w_second(i, o):
        piece = w_piece(i, line_start, 512)
        return remote(piece, piece, w_second_sem.at[i - 1], o - 1, second_peer(o))

    def w_second_arrived(i, o):
        piece = w_piece(i, half_rows + lax.rem(second_place + 4 - o, 4) * 512, 512)
        remote(piece, piece, w_second_sem.at[i - 1], o - 1, second_peer(o)).wait_recv()

    def w_core(i):
        piece = w_piece(i, half_rows, 2048)
        return remote(piece, piece, w_core_sem, i - 1, other)

    def w_core_arrived(i):
        piece = w_piece(i, 2048 - half_rows, 2048)
        remote(piece, piece, w_core_sem, i - 1, other).wait_recv()

    def features(rows_ref, feat_ref, h):
        def chunk(p, _):
            phase = dot(rows_ref[tile_rows(p), columns(h)], freq_ref[h])
            cosine, sine = cos_sin(phase)
            feat_ref[h, tile_rows(p), 0:128] = cosine.astype(BF16)
            feat_ref[h, tile_rows(p), 128:256] = sine.astype(BF16)
            return 0

        lax.fori_loop(0, PIECES, chunk, 0)

    def head_rows(h):
        return pl.ds(pl.multiple_of(h * HDIM, HDIM), HDIM)

    def part(i):
        return pl.ds(pl.multiple_of(i * PART, PART), PART)

    def key_side(h, _):
        features(k_ref, kf, h)
        for b in (0, 1):
            rows = slice(b * BLOCK, (b + 1) * BLOCK)
            state[b, head_rows(h), :] = dot(v_ref[rows, columns(h)], kf[h, rows, :], ((0,), (0,)))
        total[head_rows(h), :] = (state[0, head_rows(h), :] + state[1, head_rows(h), :]).astype(BF16)
        return 0

    def send_part(i):
        return pltpu.make_async_remote_copy(
            src_ref=total.at[part(i), :], dst_ref=parts.at[seat],
            send_sem=parts_sem.at[0, i], recv_sem=parts_sem.at[1, seat],
            device_id={"ctx": row_seat(i), "head": me}, device_id_type=MESH,
        )

    def part_arrived(i):
        i = lax.rem(seat + i, SEATS)
        pltpu.make_async_remote_copy(
            src_ref=parts.at[i], dst_ref=parts.at[i],
            send_sem=parts_sem.at[0, i], recv_sem=parts_sem.at[1, i],
            device_id={"ctx": row_seat(i), "head": me}, device_id_type=MESH,
        ).wait_recv()

    def send_sum(i):
        return pltpu.make_async_remote_copy(
            src_ref=sums.at[i], dst_ref=low.at[0, part(seat), :],
            send_sem=sums_sem.at[0, i], recv_sem=sums_sem.at[1, seat],
            device_id={"ctx": row_seat(i), "head": me}, device_id_type=MESH,
        )

    def sum_arrived(i):
        i = lax.rem(seat + i, SEATS)
        piece = low.at[0, part(i), :]
        pltpu.make_async_remote_copy(
            src_ref=piece, dst_ref=piece,
            send_sem=sums_sem.at[0, i], recv_sem=sums_sem.at[1, i],
            device_id={"ctx": row_seat(i), "head": me}, device_id_type=MESH,
        ).wait_recv()

    def to_others(start, first, last):
        def step(i, _):
            @pl.when(i != seat)
            def _():
                start(i)

            return 0

        lax.fori_loop(first, last, step, 0)

    for load in loads[:3]:
        load.wait()
    lax.fori_loop(0, 2, key_side, 0)
    pl.semaphore_wait(barrier, 16)
    to_others(lambda i: send_part(i).start(), 0, 4)
    lax.fori_loop(2, 4, key_side, 0)
    to_others(lambda i: send_part(i).start(), 4, 8)
    for i in (1, 2, 3):
        w_z(i).start()
    parts[seat] = total[part(seat), :]

    loads[3].wait()
    loads[4].wait()

    def query_side(h, _):
        features(q_ref, qf, h)
        return 0

    lax.fori_loop(0, HEADS, query_side, 0)

    for i in range(1, SEATS):
        part_arrived(i)
    row_total = parts[0].astype(F32)
    for i in range(1, SEATS):
        row_total = row_total + parts[i].astype(F32)
    row_out[...] = row_total.astype(BF16)

    def send_row(i):
        return remote(row_out, row_in.at[i - 1], row_sem, i - 1, along_y(i))

    for i in (2, 1, 3):
        send_row(i).start()

    causal = (
        lax.broadcasted_iota(jnp.int32, (TILE, TILE), 0)
        >= lax.broadcasted_iota(jnp.int32, (TILE, TILE), 1)
    )

    def attend(n, _):
        h, b = n // 2, lax.rem(n, 2)
        upper, lower = tile_rows(2 * b), tile_rows(2 * b + 1)

        def scores(rows, cols, masked):
            s = dot(qf[h, rows, :], kf[h, cols, :], ((1,), (1,)))
            return (jnp.where(causal, s, 0.0) if masked else s).astype(BF16)

        v0, v1 = v_ref[upper, columns(h)], v_ref[lower, columns(h)]
        local[upper, columns(h)] = dot(scores(upper, upper, True), v0)
        local[lower, columns(h)] = dot(scores(lower, upper, False), v0) + dot(
            scores(lower, lower, True), v1
        )
        return 0

    lax.fori_loop(0, 3, attend, 0)

    for i in (1, 2, 3):
        send_row(i).wait()
    running = jnp.zeros((PART, FEATS), F32)
    for i in (1, 2, 3):
        running = running + jnp.where(y >= i, row_in[i - 1].astype(F32), 0.0)
    for i in range(SEATS):
        sums[i] = running.astype(BF16)
        if i < SEATS - 1:
            running = running + parts[i].astype(F32)
    to_others(lambda i: send_sum(i).start(), 0, 8)
    low[0, part(seat), :] = sums[seat]
    for i in (1, 2, 3):
        w_z_arrived(i)
        for o in (2, 1, 3):
            w_first(i, o).start()
    lax.fori_loop(3, 8, attend, 0)
    for i in range(1, SEATS):
        sum_arrived(i)
    low[1] = (low[0].astype(F32) + state[0]).astype(BF16)

    def half(q, t):
        return pl.ds(pl.multiple_of(q * TILE + t * HALF, HALF), HALF)

    def stored(slot, t):
        return full.at[lax.rem(slot + RING, RING), t * HALF : (t + 1) * HALF, :]

    def to_pair(t, k):
        target = mate if k == 0 else lax.rem(me + sign * {1: -1, 2: 2, 3: -3}[k] + RING, RING)
        piece = normed.at[half(target // 2, t), :]
        return remote_z(piece, stored(me, t), rows_sem.at[t], k, target)

    def rows_arrived(t, k):
        piece = stored(mate if k == 0 else me - sign * k, t)
        remote_z(piece, piece, rows_sem.at[t], k, mate).wait_recv()

    def pass_on(t, k):
        piece = stored(me - sign * k, t)
        return remote_z(piece, piece, pass_sem.at[t], k - 1, mate)

    def forward(t, k):
        rows_arrived(t, k)
        pass_on(t, k).start()

    def passed(t):
        for k in (1, 2, 3):
            piece = stored(me + sign * (k + 1), t)
            remote_z(piece, piece, pass_sem.at[t], k - 1, mate).wait_recv()

    def finish(q):
        rows = tile_rows(q)
        for h in range(HEADS):
            cols = slice(h * HDIM, (h + 1) * HDIM)
            attended = local[rows, cols] + dot(
                qf[h, rows, :], low[q // 2, h * HDIM : (h + 1) * HDIM, :], ((1,), (1,))
            )
            square = jnp.mean(attended * attended, axis=-1, keepdims=True)
            gain = gain_ref[cols].astype(F32).reshape(1, HDIM)
            normed[rows, cols] = (attended * lax.rsqrt(square + 1e-06) * gain).astype(BF16)

    def line(i):
        for o in (1, 2, 3):
            w_first_arrived(i, o)
        for o in (2, 1, 3):
            w_second(i, o).start()

    def halves(i):
        for o in (1, 2, 3):
            w_second_arrived(i, o)
        w_core(i).start()

    def project(slot, target, t):
        rows = slice(t * HALF, (t + 1) * HALF)
        for s in (0, 2, 4, 6):
            term = dot(full[s, rows, :], w_ref[slot, s * 512 : s * 512 + 512, :]) + dot(
                full[s + 1, rows, :], w_ref[slot, s * 512 + 512 : s * 512 + 1024, :]
            )
            if s == 0:
                acc[...] = term
            elif s < 6:
                acc[...] += term
            else:
                out_ref[target, rows, :] = (acc[...] + term).astype(BF16)

    def back(t, i):
        return remote_z(
            out_ref.at[i, t * HALF : (t + 1) * HALF, :], out_hbm.at[half(pair, t), :],
            back_sem.at[t], i - 1, member(slot_of(i)),
        )

    def back_arrived(t, i):
        r = lax.rem(pair + i, 4)
        piece = out_hbm.at[half(r, t), :]
        remote_z(
            out_ref.at[i, t * HALF : (t + 1) * HALF, :], piece, back_sem.at[t], i - 1, member(r)
        ).wait_recv()

    def give_back(t, i):
        project(slot_of(i), i, t)
        back(t, i).start()

    line(1)
    for k, step in ((3, 2), (2, sign), (1, -sign), (0, 0)):
        finish(lax.rem(pair + step + 4, 4))
        to_pair(0, k).start()
    to_pair(1, 0).start()
    full[me] = normed[tile_rows(pair), :]

    forward(0, 1)
    forward(0, 2)
    line(2)
    line(3)
    forward(0, 3)
    for k in (3, 2, 1):
        to_pair(1, k).start()
    rows_arrived(0, 0)
    halves(1)
    passed(0)
    w_core_arrived(1)
    give_back(0, 1)
    forward(1, 1)
    halves(2)
    w_core_arrived(2)
    give_back(0, 2)
    forward(1, 2)
    loads[5].wait()
    project(pair, 0, 0)
    forward(1, 3)
    halves(3)
    rows_arrived(1, 0)
    w_core_arrived(3)
    give_back(0, 3)
    passed(1)
    for i in (1, 2, 3):
        give_back(1, i)
    project(pair, 0, 1)
    keep = pltpu.make_async_copy(out_ref.at[0], out_hbm.at[tile_rows(pair), :], load_sem.at[0])
    keep.start()

    for i in (1, 2, 3):
        w_z(i).wait_send()
        w_core(i).wait_send()
        for o in (1, 2, 3):
            w_first(i, o).wait_send()
            w_second(i, o).wait_send()
    for t in (0, 1):
        for k in (1, 2, 3):
            pass_on(t, k).wait_send()
        for k in (0, 1, 2, 3):
            to_pair(t, k).wait_send()
    to_others(lambda i: send_part(i).wait_send(), 0, 8)
    to_others(lambda i: send_sum(i).wait_send(), 0, 8)
    keep.wait()
    for t in (0, 1):
        for i in (1, 2, 3):
            back(t, i).wait_send()
            back_arrived(t, i)


def local(query_rows, key_rows, value_rows, frequencies, norm_gain, out_weight):
    anywhere = pl.BlockSpec(memory_space=pl.ANY)
    operands = [
        pltpu.with_memory_space_constraint(operand, pltpu.HBM)
        for operand in (query_rows, key_rows, value_rows, frequencies, norm_gain, out_weight)
    ]
    return pl.pallas_call(
        kernel,
        out_shape=jax.ShapeDtypeStruct((ROWS, 512), BF16),
        in_specs=[anywhere] * 6,
        out_specs=anywhere,
        scratch_shapes=[
            pltpu.VMEM((ROWS, 512), BF16),
            pltpu.VMEM((ROWS, 512), BF16),
            pltpu.VMEM((ROWS, 512), BF16),
            pltpu.VMEM((HEADS, HDIM, HDIM), BF16),
            pltpu.VMEM((512,), BF16),
            pltpu.VMEM((4, 4096, 512), BF16),
            pltpu.VMEM((HEADS, ROWS, FEATS), BF16),
            pltpu.VMEM((HEADS, ROWS, FEATS), BF16),
            pltpu.VMEM((2, 512, FEATS), F32),
            pltpu.VMEM((ROWS, 512), F32),
            pltpu.VMEM((ROWS, 512), BF16),
            pltpu.VMEM((RING, TILE, 512), BF16),
            pltpu.VMEM((HALF, 512), F32),
            pltpu.VMEM((4, TILE, 512), BF16),
            pltpu.VMEM((512, FEATS), BF16),
            pltpu.VMEM((SEATS, PART, FEATS), BF16),
            pltpu.VMEM((PART, FEATS), BF16),
            pltpu.VMEM((3, PART, FEATS), BF16),
            pltpu.VMEM((SEATS, PART, FEATS), BF16),
            pltpu.VMEM((2, 512, FEATS), BF16),
            pltpu.SemaphoreType.DMA((6,)),
            pltpu.SemaphoreType.DMA((2, SEATS)),
            pltpu.SemaphoreType.DMA((2, 3)),
            pltpu.SemaphoreType.DMA((2, SEATS)),
            pltpu.SemaphoreType.DMA((2, 3)),
            pltpu.SemaphoreType.DMA((3, 2, 3)),
            pltpu.SemaphoreType.DMA((3, 2, 3)),
            pltpu.SemaphoreType.DMA((2, 3)),
            pltpu.SemaphoreType.DMA((2, 2, 4)),
            pltpu.SemaphoreType.DMA((2, 2, 3)),
            pltpu.SemaphoreType.DMA((2, 2, 3)),
        ],
        compiler_params=pltpu.CompilerParams(
            collective_id=0, has_side_effects=True, vmem_limit_bytes=50 * 2**20
        ),
        cost_estimate=pl.CostEstimate(
            flops=7 * 10**9, bytes_accessed=9 * 2**20, transcendentals=0
        ),
    )(*operands)


def solution(mesh):
    return jax.shard_map(
        local,
        mesh=mesh,
        in_specs=(
            P("ctx", "head"),
            P("ctx", "head"),
            P("ctx", "head"),
            P("head", None, None),
            P("head"),
            P(None, "head"),
        ),
        out_specs=P("ctx", "head"),
        check_vma=False,
    )
```

time: 106 us -> 92.7 us (0.87)
  the two profiles are of different devices: /device:TPU:33 before, /device:TPU:1 now
where the time goes in v3:
time: 92.7 us; the launch traced here: 91.7 us
  Pallas kernels  90.7 us (98%)
  local copies, waits for them, and re-layouts  0.97 us (1%)
    pallas_call x1, Pallas kernels, local(): pl.pallas_call(kernel, out_shape=jax.ShapeDtypeStruct((ROWS, 512), BF16),...  90.7 us

profile of v3, /device:TPU:1, one launch (start us, length us, event | category | flops | bytes accessed | tf_op | source)
XLA Modules:
  0.0 91.7 jit_solution(16676944225537445802)
XLA Ops:
  0.0 90.7 %shard_map.64 = bf16[1024,512]{1,0:T(8,128)(2,1)S(1)} custom-call(bf16[1024,512]{1,0:T(8,128)(2,1)} %q_hbm.1, bf16[1024,512]{1,0:T(8,128)(2,1)} %k_hbm.1, bf16[1024,512]{1,0:T(8,128)(2,1)} %v_hbm.1, bf16[4,128,128]{2,1,0:T(8,128)(2,1)} %freq_hbm.1, bf16[512]{0:T(512)(128)(2,1)} %gain_hbm.1, bf16[4096,512]{1,0:T(8,128)(2,1)} %w_hbm.1), custom_call_target="tpu_custom_call" | custom-call | flops 7000000000 | bytes 9437184 | tf_op jit(solution)/shard_map/pallas_call | solution.py:486
  90.7 1.0 %copy.8 = bf16[1024,512]{1,0:T(8,128)(2,1)} copy(bf16[1024,512]{1,0:T(8,128)(2,1)S(1)} %shard_map.64) | data formatting | bytes 2097152

commit v4 on v3

--- a/solution.py
+++ b/solution.py
@@ -82,7 +82,7 @@
     q_ref, k_ref, v_ref, freq_ref, gain_ref, w_ref, qf, kf, state, local, normed, full, acc, out_ref,
     total, parts, row_out, row_in, sums, low,
     load_sem, parts_sem, row_sem, sums_sem,
-    w_z_sem, w_first_sem, w_second_sem, w_core_sem, rows_sem, pass_sem, back_sem,
+    w_z_sem, w_first_sem, w_second_sem, w_relay_sem, w_core_sem, rows_sem, pass_sem, back_sem,
 ):
     ctx = lax.axis_index("ctx")
     me = lax.axis_index("head")
@@ -191,13 +191,23 @@
         piece = w_piece(i, half_rows + lax.rem(second_place + 4 - o, 4) * 512, 512)
         remote(piece, piece, w_second_sem.at[i - 1], o - 1, second_peer(o)).wait_recv()
 
-    def w_core(i):
-        piece = w_piece(i, half_rows, 2048)
-        return remote(piece, piece, w_core_sem, i - 1, other)
+    def w_relay(i, d):
+        source = lax.rem(second_place + (3 if d == 0 else 1), 4)
+        piece = w_piece(i, half_rows + source * 512 + d * 256, 256)
+        return remote(piece, piece, w_relay_sem.at[i - 1], d, second_peer(1 if d == 0 else 3))
+
+    def w_relay_arrived(i, d):
+        piece = w_piece(i, half_rows + lax.rem(second_place + 2, 4) * 512 + d * 256, 256)
+        remote(piece, piece, w_relay_sem.at[i - 1], d, second_peer(1)).wait_recv()
+
+    def w_core(i, o):
+        piece = w_piece(i, half_rows + lax.rem(second_place + 4 - o, 4) * 512, 512)
+        return remote(piece, piece, w_core_sem.at[i - 1], o, other)
 
     def w_core_arrived(i):
-        piece = w_piece(i, 2048 - half_rows, 2048)
-        remote(piece, piece, w_core_sem, i - 1, other).wait_recv()
+        for o in (0, 1, 2, 3):
+            piece = w_piece(i, 2048 - half_rows + o * 512, 512)
+            remote(piece, piece, w_core_sem.at[i - 1], o, other).wait_recv()
 
     def features(rows_ref, feat_ref, h):
         def chunk(p, _):
@@ -207,7 +217,7 @@
             feat_ref[h, tile_rows(p), 128:256] = sine.astype(BF16)
             return 0
 
-        lax.fori_loop(0, PIECES, chunk, 0)
+        lax.fori_loop(0, PIECES, chunk, 0, unroll=True)
 
     def head_rows(h):
         return pl.ds(pl.multiple_of(h * HDIM, HDIM), HDIM)
@@ -381,13 +391,20 @@
     def line(i):
         for o in (1, 2, 3):
             w_first_arrived(i, o)
-        for o in (2, 1, 3):
+        for o in (1, 3):
             w_second(i, o).start()
+        w_core(i, 0).start()
+
+    def relay(i):
+        for d, o in ((0, 1), (1, 3)):
+            w_second_arrived(i, o)
+            w_relay(i, d).start()
+            w_core(i, o).start()
 
     def halves(i):
-        for o in (1, 2, 3):
-            w_second_arrived(i, o)
-        w_core(i).start()
+        for d in (0, 1):
+            w_relay_arrived(i, d)
+        w_core(i, 2).start()
 
     def project(slot, target, t):
         rows = slice(t * HALF, (t + 1) * HALF)
@@ -426,13 +443,15 @@
     to_pair(1, 0).start()
     full[me] = normed[tile_rows(pair), :]
 
+    line(2)
+    line(3)
     forward(0, 1)
     forward(0, 2)
-    line(2)
-    line(3)
     forward(0, 3)
     for k in (3, 2, 1):
         to_pair(1, k).start()
+    for i in (1, 2, 3):
+        relay(i)
     rows_arrived(0, 0)
     halves(1)
     passed(0)
@@ -459,10 +478,13 @@
 
     for i in (1, 2, 3):
         w_z(i).wait_send()
-        w_core(i).wait_send()
+        for o in (0, 1, 2, 3):
+            w_core(i, o).wait_send()
         for o in (1, 2, 3):
             w_first(i, o).wait_send()
+        for d, o in ((0, 1), (1, 3)):
             w_second(i, o).wait_send()
+            w_relay(i, d).wait_send()
     for t in (0, 1):
         for k in (1, 2, 3):
             pass_on(t, k).wait_send()
@@ -516,7 +538,8 @@
             pltpu.SemaphoreType.DMA((2, 3)),
             pltpu.SemaphoreType.DMA((3, 2, 3)),
             pltpu.SemaphoreType.DMA((3, 2, 3)),
-            pltpu.SemaphoreType.DMA((2, 3)),
+            pltpu.SemaphoreType.DMA((3, 2, 2)),
+            pltpu.SemaphoreType.DMA((3, 2, 4)),
             pltpu.SemaphoreType.DMA((2, 2, 4)),
             pltpu.SemaphoreType.DMA((2, 2, 3)),
             pltpu.SemaphoreType.DMA((2, 2, 3)),

time: 92.7 us -> 88.4 us (0.954)
  the two profiles are of different devices: /device:TPU:1 before, /device:TPU:6 now
where the time goes in v4:
time: 88.4 us; the launch traced here: 88.3 us
  Pallas kernels  87.3 us (99%)
  local copies, waits for them, and re-layouts  0.97 us (1%)
    pallas_call x1, Pallas kernels, local(): pl.pallas_call(kernel, out_shape=jax.ShapeDtypeStruct((ROWS, 512), BF16),...  87.3 us

profile of v4, /device:TPU:6, one launch (start us, length us, event | category | flops | bytes accessed | tf_op | source)
XLA Modules:
  0.0 88.3 jit_solution(6971569056939203791)
XLA Ops:
  0.0 87.3 %shard_map.64 = bf16[1024,512]{1,0:T(8,128)(2,1)S(1)} custom-call(bf16[1024,512]{1,0:T(8,128)(2,1)} %q_hbm.1, bf16[1024,512]{1,0:T(8,128)(2,1)} %k_hbm.1, bf16[1024,512]{1,0:T(8,128)(2,1)} %v_hbm.1, bf16[4,128,128]{2,1,0:T(8,128)(2,1)} %freq_hbm.1, bf16[512]{0:T(512)(128)(2,1)} %gain_hbm.1, bf16[4096,512]{1,0:T(8,128)(2,1)} %w_hbm.1), custom_call_target="tpu_custom_call" | custom-call | flops 7000000000 | bytes 9437184 | tf_op jit(solution)/shard_map/pallas_call | solution.py:508
  87.3 1.0 %copy.8 = bf16[1024,512]{1,0:T(8,128)(2,1)} copy(bf16[1024,512]{1,0:T(8,128)(2,1)S(1)} %shard_map.64) | data formatting | bytes 2097152

commit v5 on v4

--- a/solution.py
+++ b/solution.py
@@ -448,23 +448,24 @@
     forward(0, 1)
     forward(0, 2)
     forward(0, 3)
+    relay(1)
     for k in (3, 2, 1):
         to_pair(1, k).start()
-    for i in (1, 2, 3):
-        relay(i)
+    relay(2)
+    relay(3)
     rows_arrived(0, 0)
     halves(1)
     passed(0)
+    forward(1, 1)
+    forward(1, 2)
     w_core_arrived(1)
     give_back(0, 1)
-    forward(1, 1)
     halves(2)
+    forward(1, 3)
     w_core_arrived(2)
     give_back(0, 2)
-    forward(1, 2)
     loads[5].wait()
     project(pair, 0, 0)
-    forward(1, 3)
     halves(3)
     rows_arrived(1, 0)
     w_core_arrived(3)

time: 88.4 us -> 87.8 us (level)
  the two profiles are of different devices: /device:TPU:6 before, /device:TPU:1 now
where the time goes in v5:
time: 87.8 us
  Pallas kernels  86.8 us (99%)
  local copies, waits for them, and re-layouts  0.97 us (1%)
    pallas_call x1, Pallas kernels, local(): pl.pallas_call(kernel, out_shape=jax.ShapeDtypeStruct((ROWS, 512), BF16),...  86.8 us

profile of v5, /device:TPU:1, one launch (start us, length us, event | category | flops | bytes accessed | tf_op | source)
XLA Modules:
  0.0 87.8 jit_solution(7042801506849521191)
XLA Ops:
  0.0 86.8 %shard_map.64 = bf16[1024,512]{1,0:T(8,128)(2,1)S(1)} custom-call(bf16[1024,512]{1,0:T(8,128)(2,1)} %q_hbm.1, bf16[1024,512]{1,0:T(8,128)(2,1)} %k_hbm.1, bf16[1024,512]{1,0:T(8,128)(2,1)} %v_hbm.1, bf16[4,128,128]{2,1,0:T(8,128)(2,1)} %freq_hbm.1, bf16[512]{0:T(512)(128)(2,1)} %gain_hbm.1, bf16[4096,512]{1,0:T(8,128)(2,1)} %w_hbm.1), custom_call_target="tpu_custom_call" | custom-call | flops 7000000000 | bytes 9437184 | tf_op jit(solution)/shard_map/pallas_call | solution.py:509
  86.8 1.0 %copy.8 = bf16[1024,512]{1,0:T(8,128)(2,1)} copy(bf16[1024,512]{1,0:T(8,128)(2,1)S(1)} %shard_map.64) | data formatting | bytes 2097152

commit v6 on v5

--- a/solution.py
+++ b/solution.py
@@ -440,7 +440,6 @@
     for k, step in ((3, 2), (2, sign), (1, -sign), (0, 0)):
         finish(lax.rem(pair + step + 4, 4))
         to_pair(0, k).start()
-    to_pair(1, 0).start()
     full[me] = normed[tile_rows(pair), :]
 
     line(2)
@@ -449,7 +448,7 @@
     forward(0, 2)
     forward(0, 3)
     relay(1)
-    for k in (3, 2, 1):
+    for k in (3, 2, 1, 0):
         to_pair(1, k).start()
     relay(2)
     relay(3)

time: 87.8 us -> 91.6 us (1.043)
  Pallas kernels: 86.8 us -> 90.5 us
    pallas_call x1, Pallas kernels: 86.8 us -> 90.5 us  [local(): pl.pallas_call(kernel, out_shape=jax.ShapeDtypeStruct((ROWS, 512), BF16),...]
where the time goes in v6:
time: 91.6 us; the launch traced here: 91.5 us
  Pallas kernels  90.5 us (99%)
  local copies, waits for them, and re-layouts  0.97 us (1%)
    pallas_call x1, Pallas kernels, local(): pl.pallas_call(kernel, out_shape=jax.ShapeDtypeStruct((ROWS, 512), BF16),...  90.5 us

profile of v6, /device:TPU:1, one launch (start us, length us, event | category | flops | bytes accessed | tf_op | source)
XLA Modules:
  0.0 91.5 jit_solution(3040569001647293035)
XLA Ops:
  0.0 90.5 %shard_map.64 = bf16[1024,512]{1,0:T(8,128)(2,1)S(1)} custom-call(bf16[1024,512]{1,0:T(8,128)(2,1)} %q_hbm.1, bf16[1024,512]{1,0:T(8,128)(2,1)} %k_hbm.1, bf16[1024,512]{1,0:T(8,128)(2,1)} %v_hbm.1, bf16[4,128,128]{2,1,0:T(8,128)(2,1)} %freq_hbm.1, bf16[512]{0:T(512)(128)(2,1)} %gain_hbm.1, bf16[4096,512]{1,0:T(8,128)(2,1)} %w_hbm.1), custom_call_target="tpu_custom_call" | custom-call | flops 7000000000 | bytes 9437184 | tf_op jit(solution)/shard_map/pallas_call | solution.py:508
  90.5 1.0 %copy.8 = bf16[1024,512]{1,0:T(8,128)(2,1)} copy(bf16[1024,512]{1,0:T(8,128)(2,1)S(1)} %shard_map.64) | data formatting | bytes 2097152
